TPU v7x, 128 devices: a whole 4x4x4 slice. The times are simulated.
128 devices in a mesh: dp: 4 (over x_lo, core), code: 32 (over z, y, x_hi).
Axes of the slice: x: 4 (x_hi: 2, x_lo: 2; x = x_hi * 2 + x_lo), y: 4, z: 4, core: 2. Of those that a mesh axis runs over, the one named last changes fastest.
Arguments:
- image_tokens: bfloat16 [16384, 1024], P(('dp', 'code')), may hold values from -6 to 6
- w_in: bfloat16 [1024, 4096], replicated, as said below
- w_out: bfloat16 [4096, 1024], replicated, as said below
- w_proj: bfloat16 [1024, 256], replicated, as said below
- codebook: bfloat16 [131072, 256], P('code'), may hold values from -6 to 6
- inv_temp: float32 [16384], replicated, may hold values from 4 to 240, as said below
- prior_mass: float32 [131072], P('code'), may hold values from 0.02 to 0.2
Outputs:
- refit_codes: float32 [131072, 256], P(('code', 'dp'))
- code_mass: float32 [131072], P(('code', 'dp'))
Inputs may be any that keep to these rules, and one draw needn't show every extreme that they name: `inv_temp`: positive inverse temperatures. `w_in`: every entry lies within 6 / sqrt(1024) of zero. `w_out`: every entry lies within 6 / sqrt(4096) of zero. `w_proj`: every entry lies within 6 / sqrt(1024) of zero.
All inputs are finite; a program needn't handle non-finite values.
Results may differ from a plain program's by a relative error of at most 0.003.
The roundings to bfloat16 on the way count: a program that leaves them out, or rounds other values in their place, can miss the bound.
Values may be sent and summed in bfloat16 or wider, within the bound.
A program may use at most 128 MiB of HBM per device.

v0:
```python
import math
import jax
import jax.numpy as jnp
from jax import lax
from jax.sharding import PartitionSpec as P


def encode(image_tokens, w_in, w_out, w_proj):
    tokens_f = image_tokens.astype(jnp.float32)
    mean = jnp.mean(tokens_f, axis=1, keepdims=True)
    centered = tokens_f - mean
    var = jnp.mean(centered * centered, axis=1, keepdims=True)
    normed = (centered * lax.rsqrt(var + 1e-06)).astype(jnp.bfloat16)
    hidden = jax.nn.gelu(
        jnp.dot(normed, w_in, preferred_element_type=jnp.float32), approximate=False
    ).astype(jnp.bfloat16)
    encoded = (tokens_f + jnp.dot(hidden, w_out, preferred_element_type=jnp.float32)).astype(
        jnp.bfloat16
    )
    projected = jnp.dot(encoded, w_proj, preferred_element_type=jnp.float32)
    width = projected.shape[1]
    factor = jnp.sqrt(width / (jnp.sum(projected * projected, axis=1, keepdims=True) + 1e-06))
    return (projected * factor).astype(jnp.bfloat16)


def in_blocks(func, arrays):
    rows = arrays[0].shape[0]
    block = math.gcd(rows, 512)
    shaped = tuple((item.reshape((rows // block, block) + item.shape[1:]) for item in arrays))
    results = lax.map(lambda items: func(*items), shaped)
    return jax.tree.map(lambda item: item.reshape((rows,) + item.shape[2:]), results)


def weighted_sums(token_rows, scale_rows, norm_rows, code_rows):
    rows = token_rows.shape[0]
    width = token_rows.shape[1]
    block = math.gcd(rows, 512)
    count = rows // block

    def accumulate(carry, items):
        token_block, scale_block, norm_block = items
        logits = (
            jnp.dot(token_block, code_rows.T, preferred_element_type=jnp.float32)
            * scale_block[:, None]
        )
        resp = jnp.exp(logits - norm_block[:, None]).astype(jnp.bfloat16)
        sums = carry[0] + lax.dot_general(
            resp, token_block, (((0,), (0,)), ((), ())), preferred_element_type=jnp.float32
        )
        mass = carry[1] + jnp.sum(resp.astype(jnp.float32), axis=0)
        return ((sums, mass), None)

    start = (
        jnp.zeros((code_rows.shape[0], width), jnp.float32),
        jnp.zeros((code_rows.shape[0],), jnp.float32),
    )
    items = (
        token_rows.reshape(count, block, width),
        scale_rows.reshape(count, block),
        norm_rows.reshape(count, block),
    )
    (sums, mass), _ = lax.scan(accumulate, start, items)
    return (sums, mass)


def local(image_tokens, w_in, w_out, w_proj, codebook, inv_temp, prior_mass):
    unit_tokens = encode(image_tokens, w_in, w_out, w_proj)
    width = unit_tokens.shape[1]
    codebook_f = codebook.astype(jnp.float32)
    unit_codes = (
        codebook_f * lax.rsqrt(jnp.mean(codebook_f * codebook_f, axis=1, keepdims=True) + 1e-06)
    ).astype(jnp.bfloat16)
    group_rows = unit_tokens.shape[0] * lax.axis_size("code")
    group_index = lax.axis_index("dp")
    all_scale = inv_temp * (1.0 / width)
    group_scale = lax.dynamic_slice_in_dim(all_scale, group_index * group_rows, group_rows)

    def block_stats(token_block, scale_block):
        logits = (
            jnp.dot(token_block, unit_codes.T, preferred_element_type=jnp.float32)
            * scale_block[:, None]
        )
        peak = jnp.max(logits, axis=1)
        return (peak, jnp.sum(jnp.exp(logits - peak[:, None]), axis=1))

    piece = lax.all_gather(unit_tokens, "code", axis=0, tiled=True)
    peak, total = in_blocks(block_stats, (piece, group_scale))
    local_peak = peak
    local_total = total
    peak = lax.pmax(local_peak, "code")
    total = lax.psum(local_total * jnp.exp(local_peak - peak), "code")
    lognorm = peak + jnp.log(total)
    owned = codebook.shape[0] // lax.axis_size("dp")
    sums, mass = weighted_sums(piece, group_scale, lognorm, unit_codes)
    sums, mass = (
        lax.psum_scatter(sums, "dp", scatter_dimension=0, tiled=True),
        lax.psum_scatter(mass, "dp", scatter_dimension=0, tiled=True),
    )
    own_book = lax.dynamic_slice_in_dim(codebook_f, group_index * owned, owned)
    own_prior = lax.dynamic_slice_in_dim(prior_mass, group_index * owned, owned)
    refit = (own_prior[:, None] * own_book + sums) / (own_prior + mass)[:, None]
    return (refit, mass)


def solution(mesh):
    placed = (P(("dp", "code"), None), P(), P(), P(), P("code", None), P(), P("code"))
    return jax.shard_map(
        local,
        mesh=mesh,
        in_specs=placed,
        out_specs=(P(("code", "dp"), None), P(("code", "dp"))),
        check_vma=False,
    )
```

profile of v0, /device:TPU:1, one launch (start us, length us, event | category | flops | bytes accessed | tf_op | source)
XLA Modules:
  0.0 665.6 jit_solution(4588213453708250442)
XLA Ops:
  10.5 6.2 fusion.28
  38.5 18.3 %multiply_reduce_fusion.2 = (f32[128]{0:T(128)S(1)}, f32[128,256]{1,0:T(8,128)S(1)}) fusion(bf16[1024,256]{1,0:T(8,128)(2,1)S(1)} %copy-done, f32[128,1024]{1,0:T(8,128)S(1)} %convert_element_type.28, bf16[4096,1024]{1,0:T(8,128)(2,1)} %param.13, f32[128,4096]{1,0:T(8,128)} %erfc.292, f32[128,4096]{1,0:T(8,128)} %erfc.290, f32[128,4096]{1,0:T(8,128)} %erfc.301, ...), kind=kOutput, calls=%fused_computation.54 | convolution fusion | flops 1175256960 | bytes 41026048 | tf_op jit(solution)/shard_map/dot_general | solution.py:20
  60.9 68.3 %all-gather.2.cloned.1.call-done = bf16[4096,256]{1,0:T(8,128)(2,1)} async-done(((bf16[128,256]{1,0:T(8,128)(2,1)}), bf16[4096,256]{1,0:T(8,128)(2,1)}) %all-gather.2.cloned.1.call-update) | async-done | bytes 2097168 | tf_op jit(solution)/shard_map/all_gather | solution.py:86
  129.2 34.2 %while.25 = (s32[]{:T(128)}, f32[8,512]{1,0:T(8,128)S(1)}, f32[8,512]{1,0:T(8,128)S(1)}, bf16[8,512,256]{2,1,0:T(8,128)(2,1)}, bf16[4096,256]{1,0:T(8,128)(2,1)S...) while((s32[]{:T(128)}, f32[8,512]{1,0:T(8,128)S(1)}, f32[8,512]{1,0:T(8,128)S(1)}, ...), condition=%wide.region_7.8_spmd, body=%wide.region_4.7_spmd.sunk | while | flops 1084226560 | bytes 19159648 | solution.py:30
  133.5 2.3 multiply_reduce_fusion.4
  137.8 2.3 multiply_reduce_fusion.4
  142.1 2.3 multiply_reduce_fusion.4
  146.3 2.3 multiply_reduce_fusion.4
  150.6 2.3 multiply_reduce_fusion.4
  154.9 2.3 multiply_reduce_fusion.4
  163.5 153.2 %pmax.7 = f32[4096]{0:T(1024)S(1)} all-reduce(f32[4096]{0:T(1024)S(1)} %bitcast.56), channel_id=1, replica_groups=mesh['dp'=4,'code'=32] {'code'}, use_global_device_ids=true, to_apply=%region_8.9 | all-reduce | flops 4096 | bytes 32768 | tf_op jit(solution)/shard_map/pmax | solution.py:90
  316.7 149.6 %psum.7 = f32[4096]{0:T(1024)S(1)} all-reduce(f32[4096]{0:T(1024)S(1)} %exponential_multiply_fusion), channel_id=1, replica_groups=mesh['dp'=4,'code'=32] {'code'}, use_global_device_ids=true, to_apply=%region_9.10 | all-reduce | flops 4096 | bytes 32768 | tf_op jit(solution)/shard_map/psum | solution.py:91
  466.3 91.9 %while.26 = (s32[]{:T(128)}, f32[4096,256]{1,0:T(8,128)}, f32[4096]{0:T(1024)S(1)}, bf16[8,512,256]{2,1,0:T(8,128)(2,1)}, bf16[4096,256]{1,0:T(8,128)(2,1)S(1)},...) while((s32[]{:T(128)}, f32[4096,256]{1,0:T(8,128)}, ...), condition=%wide.region_12.13_spmd.clone, body=%wide.region_10.12_spmd.clone.sunk | while | flops 2160070656 | bytes 19477612 | solution.py:62
  466.3 4.9 convert_reduce_fusion.3
  471.2 5.4 convolution_add_fusion.3
  476.7 4.9 convert_reduce_fusion.3
  481.5 6.8 %convolution_add_fusion.3 = f32[4096,256]{1,0:T(8,128)} fusion(bf16[512,4096]{1,0:T(8,128)(2,1)} %get-tuple-element.228, f32[4096,256]{1,0:T(8,128)} %get-tuple-element.264, pred[]{:T(512)S(6)} %compare.3, bf16[8,512,256]{2,1,0:T(8,128)(2,1)} %get-tuple-element.275, s32[]{:T(128)} %get-tuple-element.263), kind=kOutput, calls=%fused_computation.9.clone.1 | convolution fusion | flops 1075838976 | bytes 12845569 | tf_op jit(solution)/shard_map/while/body/eval_jaxpr/dot_general | solution.py:47
  488.3 4.9 convert_reduce_fusion.3
  493.2 6.8 %convolution_add_fusion.3 = f32[4096,256]{1,0:T(8,128)} fusion(bf16[512,4096]{1,0:T(8,128)(2,1)} %get-tuple-element.228, f32[4096,256]{1,0:T(8,128)} %get-tuple-element.264, pred[]{:T(512)S(6)} %compare.3, bf16[8,512,256]{2,1,0:T(8,128)(2,1)} %get-tuple-element.275, s32[]{:T(128)} %get-tuple-element.263), kind=kOutput, calls=%fused_computation.9.clone.1 | convolution fusion | flops 1075838976 | bytes 12845569 | tf_op jit(solution)/shard_map/while/body/eval_jaxpr/dot_general | solution.py:47
  499.9 4.9 convert_reduce_fusion.3
  504.8 6.8 %convolution_add_fusion.3 = f32[4096,256]{1,0:T(8,128)} fusion(bf16[512,4096]{1,0:T(8,128)(2,1)} %get-tuple-element.228, f32[4096,256]{1,0:T(8,128)} %get-tuple-element.264, pred[]{:T(512)S(6)} %compare.3, bf16[8,512,256]{2,1,0:T(8,128)(2,1)} %get-tuple-element.275, s32[]{:T(128)} %get-tuple-element.263), kind=kOutput, calls=%fused_computation.9.clone.1 | convolution fusion | flops 1075838976 | bytes 12845569 | tf_op jit(solution)/shard_map/while/body/eval_jaxpr/dot_general | solution.py:47
  511.6 4.9 convert_reduce_fusion.3
  516.5 6.8 %convolution_add_fusion.3 = f32[4096,256]{1,0:T(8,128)} fusion(bf16[512,4096]{1,0:T(8,128)(2,1)} %get-tuple-element.228, f32[4096,256]{1,0:T(8,128)} %get-tuple-element.264, pred[]{:T(512)S(6)} %compare.3, bf16[8,512,256]{2,1,0:T(8,128)(2,1)} %get-tuple-element.275, s32[]{:T(128)} %get-tuple-element.263), kind=kOutput, calls=%fused_computation.9.clone.1 | convolution fusion | flops 1075838976 | bytes 12845569 | tf_op jit(solution)/shard_map/while/body/eval_jaxpr/dot_general | solution.py:47
  523.2 4.9 convert_reduce_fusion.3
  528.1 6.8 %convolution_add_fusion.3 = f32[4096,256]{1,0:T(8,128)} fusion(bf16[512,4096]{1,0:T(8,128)(2,1)} %get-tuple-element.228, f32[4096,256]{1,0:T(8,128)} %get-tuple-element.264, pred[]{:T(512)S(6)} %compare.3, bf16[8,512,256]{2,1,0:T(8,128)(2,1)} %get-tuple-element.275, s32[]{:T(128)} %get-tuple-element.263), kind=kOutput, calls=%fused_computation.9.clone.1 | convolution fusion | flops 1075838976 | bytes 12845569 | tf_op jit(solution)/shard_map/while/body/eval_jaxpr/dot_general | solution.py:47
  534.9 4.9 convert_reduce_fusion.3
  539.8 6.8 %convolution_add_fusion.3 = f32[4096,256]{1,0:T(8,128)} fusion(bf16[512,4096]{1,0:T(8,128)(2,1)} %get-tuple-element.228, f32[4096,256]{1,0:T(8,128)} %get-tuple-element.264, pred[]{:T(512)S(6)} %compare.3, bf16[8,512,256]{2,1,0:T(8,128)(2,1)} %get-tuple-element.275, s32[]{:T(128)} %get-tuple-element.263), kind=kOutput, calls=%fused_computation.9.clone.1 | convolution fusion | flops 1075838976 | bytes 12845569 | tf_op jit(solution)/shard_map/while/body/eval_jaxpr/dot_general | solution.py:47
  546.5 4.9 convert_reduce_fusion.3
  551.4 6.8 %convolution_add_fusion.3 = f32[4096,256]{1,0:T(8,128)} fusion(bf16[512,4096]{1,0:T(8,128)(2,1)} %get-tuple-element.228, f32[4096,256]{1,0:T(8,128)} %get-tuple-element.264, pred[]{:T(512)S(6)} %compare.3, bf16[8,512,256]{2,1,0:T(8,128)(2,1)} %get-tuple-element.275, s32[]{:T(128)} %get-tuple-element.263), kind=kOutput, calls=%fused_computation.9.clone.1 | convolution fusion | flops 1075838976 | bytes 12845569 | tf_op jit(solution)/shard_map/while/body/eval_jaxpr/dot_general | solution.py:47
  563.3 68.3 %all-reduce = f32[4096]{0:T(1024)S(1)} all-reduce(f32[4096]{0:T(1024)S(1)} %get-tuple-element.76), channel_id=3, replica_groups=mesh['dp'=4,'code'=32] {'dp'}, use_global_device_ids=true, to_apply=%region_14.15.clone | all-reduce | flops 4096 | bytes 32768
  632.8 23.1 %reduce-scatter.2.cloned.1.call-done = f32[1024,256]{1,0:T(8,128)} async-done(((f32[4096,256]{1,0:T(8,128)}), f32[1024,256]{1,0:T(8,128)}) %reduce-scatter.2.cloned.1.call-update) | async-done | bytes 1048592 | tf_op jit(solution)/shard_map/reduce_scatter | solution.py:96
  656.0 2.8 add_divide_fusion
  (104 shorter events, 54.9 us)
Async XLA Ops:
  7.2 31.3 %copy-start = (bf16[1024,256]{1,0:T(8,128)(2,1)S(1)}, bf16[1024,256]{1,0:T(8,128)(2,1)}, u32[]{:S(2)}) copy-start(bf16[1024,256]{1,0:T(8,128)(2,1)} %param.14) | copy-start | bytes 1572868
  7.2 122.0 %all-gather.2.cloned.1.call-start = ((), (), s32[]{:S(2)}) async-start(), calls=%async_computation.1 | async-start | bytes 2162688 | tf_op jit(solution)/shard_map/all_gather | solution.py:86
  38.5 20.1 %copy-start.2 = (bf16[4096,256]{1,0:T(8,128)(2,1)S(1)}, bf16[4096,256]{1,0:T(8,128)(2,1)}, u32[]{:S(2)}) copy-start(bf16[4096,256]{1,0:T(8,128)(2,1)} %param.15) | copy-start | bytes 6291460
  57.6 598.4 %reduce-scatter.2.cloned.1.call-start = ((), (), s32[]{:S(2)}) async-start(), calls=%async_computation.2 | async-start | bytes 5242880 | tf_op jit(solution)/shard_map/reduce_scatter | solution.py:96
  58.6 1.6 copy-start.3
  558.2 1.6 copy-start.4
  559.8 2.3 copy-start.5
  559.8 99.0 %copy-start.1 = (bf16[1024,256]{1,0:T(8,128)(2,1)S(1)}, bf16[1024,256]{1,0:T(8,128)(2,1)}, u32[]{:S(2)}) copy-start(bf16[1024,256]{1,0:T(8,128)(2,1)} %param.14) | copy-start | bytes 1572868
Sparse Core Ops, SparseCore 0:
  57.7 71.4 all-gather.1
  558.3 97.5 reduce-scatter.1
where the time goes:
time: 667 us; the launch traced here: 666 us
  blocking collectives  371 us (56%)
  matrix products  135 us (20%)
  waiting for transfers between devices  91.5 us (14%)
  other arithmetic  26.8 us (4%)
  local copies, waits for them, and re-layouts  25.9 us (4%)
  between operations  14.8 us (2%)
    pmax x1, blocking collectives, local(): peak = lax.pmax(local_peak, 'code')  153 us
    psum x1, blocking collectives, local(): total = lax.psum(local_total * jnp.exp(local_peak - peak), 'code')  150 us
    all_gather x1, waiting for transfers between devices, local(): piece = lax.all_gather(unit_tokens, 'code', axis=0, tiled=True)  68.3 us
    unnamed x1, blocking collectives  68.3 us
    dot_general x8, matrix products, accumulate(): lax.dot_general(resp, token_block, (((0,), (0,)), ((), ())), preferred_el...  52.8 us
    dot_general x8, matrix products, accumulate(): jnp.dot(token_block, code_rows.T, preferred_element_type=jnp.float32)  38.9 us
    reduce_scatter x1, waiting for transfers between devices, local(): lax.psum_scatter(sums, 'dp', scatter_dimension=0, tiled=True)  23.1 us
    dot_general x8, matrix products, block_stats(): jnp.dot(token_block, unit_codes.T, preferred_element_type=jnp.float32)  18.6 us
  transfers between devices with their start and end apart: 2, of which 2 were waited for; matrix products, arithmetic and copies ran while one was open for 1% of the time, Pallas kernels for 0%

commit v1 on v0

--- a/solution.py
+++ b/solution.py
@@ -88,7 +88,9 @@
     local_peak = peak
     local_total = total
     peak = lax.pmax(local_peak, "code")
-    total = lax.psum(local_total * jnp.exp(local_peak - peak), "code")
+    part = local_total * jnp.exp(local_peak - peak)
+    parts = lax.all_gather(part, "code", axis=0, tiled=False)
+    total = parts.sum(axis=0)
     lognorm = peak + jnp.log(total)
     owned = codebook.shape[0] // lax.axis_size("dp")
     sums, mass = weighted_sums(piece, group_scale, lognorm, unit_codes)

time: 667 us -> 584 us (0.88)
  blocking collectives: 371 us -> 286 us
    psum x1 -> x0, blocking collectives: 150 us -> none  [local(): total = lax.psum(local_total * jnp.exp(local_peak - peak), 'code')]
    all_gather x0 -> x1, blocking collectives: none -> 77.5 us  [local(): parts = lax.all_gather(part, 'code', axis=0, tiled=False)]
    unnamed x1, blocking collectives: 68.3 us -> 55 us
where the time goes in v1:
time: 584 us; the launch traced here: 583 us
  blocking collectives  286 us (49%)
  matrix products  135 us (23%)
  waiting for transfers between devices  94.3 us (16%)
  other arithmetic  26.9 us (5%)
  local copies, waits for them, and re-layouts  26 us (4%)
  between operations  14.9 us (3%)
    pmax x1, blocking collectives, local(): peak = lax.pmax(local_peak, 'code')  153 us
    all_gather x1, blocking collectives, local(): parts = lax.all_gather(part, 'code', axis=0, tiled=False)  77.5 us
    all_gather x1, waiting for transfers between devices, local(): piece = lax.all_gather(unit_tokens, 'code', axis=0, tiled=True)  68.3 us
    unnamed x1, blocking collectives  55 us
    dot_general x8, matrix products, accumulate(): lax.dot_general(resp, token_block, (((0,), (0,)), ((), ())), preferred_el...  52.8 us
    dot_general x8, matrix products, accumulate(): jnp.dot(token_block, code_rows.T, preferred_element_type=jnp.float32)  38.9 us
    reduce_scatter x1, waiting for transfers between devices, local(): lax.psum_scatter(sums, 'dp', scatter_dimension=0, tiled=True)  25.9 us
    dot_general x8, matrix products, block_stats(): jnp.dot(token_block, unit_codes.T, preferred_element_type=jnp.float32)  18.6 us
  transfers between devices with their start and end apart: 2, of which 2 were waited for; matrix products, arithmetic and copies ran while one was open for 1% of the time, Pallas kernels for 0%

profile of v1, /device:TPU:1, one launch (start us, length us, event | category | flops | bytes accessed | tf_op | source)
XLA Modules:
  0.0 583.3 jit_solution(15791395720831651153)
XLA Ops:
  10.5 6.2 %fusion.28 = f32[128,4096]{1,0:T(8,128)} fusion(bf16[1024,4096]{1,0:T(8,128)(2,1)} %param.12, bf16[128,1024]{1,0:T(8,128)(2,1)} %param.11, f32[128]{0:T(128)S(1)} %add_rsqrt_fusion.1, f32[128]{0:T(128)S(1)} %broadcast_multiply_fusion), kind=kOutput, calls=%fused_computation.50 | convolution fusion | flops 1074266112 | bytes 10748928 | tf_op jit(solution)/shard_map/dot_general | solution.py:15
  38.5 18.3 %multiply_reduce_fusion.2 = (f32[128]{0:T(128)S(1)}, f32[128,256]{1,0:T(8,128)S(1)}) fusion(bf16[1024,256]{1,0:T(8,128)(2,1)S(1)} %copy-done, f32[128,1024]{1,0:T(8,128)S(1)} %convert_element_type.28, bf16[4096,1024]{1,0:T(8,128)(2,1)} %param.13, f32[128,4096]{1,0:T(8,128)} %erfc.292, f32[128,4096]{1,0:T(8,128)} %erfc.290, f32[128,4096]{1,0:T(8,128)} %erfc.301, ...), kind=kOutput, calls=%fused_computation.54 | convolution fusion | flops 1175256960 | bytes 41026048 | tf_op jit(solution)/shard_map/dot_general | solution.py:20
  60.9 68.3 %all-gather.3.cloned.1.call-done = bf16[4096,256]{1,0:T(8,128)(2,1)} async-done(((bf16[128,256]{1,0:T(8,128)(2,1)}), bf16[4096,256]{1,0:T(8,128)(2,1)}) %all-gather.3.cloned.1.call-update) | async-done | bytes 2097168 | tf_op jit(solution)/shard_map/all_gather | solution.py:86
  129.2 34.2 %while.25 = (s32[]{:T(128)}, f32[8,512]{1,0:T(8,128)S(1)}, f32[8,512]{1,0:T(8,128)S(1)}, bf16[8,512,256]{2,1,0:T(8,128)(2,1)}, bf16[4096,256]{1,0:T(8,128)(2,1)S...) while((s32[]{:T(128)}, f32[8,512]{1,0:T(8,128)S(1)}, f32[8,512]{1,0:T(8,128)S(1)}, ...), condition=%wide.region_7.8_spmd, body=%wide.region_4.7_spmd.sunk | while | flops 1084226560 | bytes 19159648 | solution.py:30
  133.5 2.3 multiply_reduce_fusion.4
  137.8 2.3 multiply_reduce_fusion.4
  142.1 2.3 multiply_reduce_fusion.4
  146.3 2.3 multiply_reduce_fusion.4
  150.6 2.3 multiply_reduce_fusion.4
  154.9 2.3 multiply_reduce_fusion.4
  163.5 153.2 %pmax.7 = f32[4096]{0:T(1024)S(1)} all-reduce(f32[4096]{0:T(1024)S(1)} %bitcast.56), channel_id=1, replica_groups=mesh['dp'=4,'code'=32] {'code'}, use_global_device_ids=true, to_apply=%region_8.9 | all-reduce | flops 4096 | bytes 32768 | tf_op jit(solution)/shard_map/pmax | solution.py:90
  316.7 77.5 %all-gather = f32[131072]{0:T(1024)S(1)} all-gather(f32[4096]{0:T(1024)S(1)} %exponential_multiply_fusion), channel_id=2, replica_groups=mesh['dp'=4,'code'=32] {'code'}, dimensions={0}, use_global_device_ids=true | all-gather | bytes 540672 | tf_op jit(solution)/shard_map/all_gather | solution.py:92
  394.4 91.9 %while.26 = (s32[]{:T(128)}, f32[4096,256]{1,0:T(8,128)}, f32[4096]{0:T(1024)S(1)}, bf16[8,512,256]{2,1,0:T(8,128)(2,1)}, bf16[4096,256]{1,0:T(8,128)(2,1)S(1)},...) while((s32[]{:T(128)}, f32[4096,256]{1,0:T(8,128)}, ...), condition=%wide.region_12.13_spmd.clone, body=%wide.region_10.12_spmd.clone.sunk | while | flops 2160070656 | bytes 19477612 | solution.py:62
  394.4 4.9 convert_reduce_fusion.3
  399.3 5.4 convolution_add_fusion.3
  404.8 4.9 convert_reduce_fusion.3
  409.6 6.8 %convolution_add_fusion.3 = f32[4096,256]{1,0:T(8,128)} fusion(bf16[512,4096]{1,0:T(8,128)(2,1)} %get-tuple-element.228, f32[4096,256]{1,0:T(8,128)} %get-tuple-element.264, pred[]{:T(512)S(6)} %compare.3, bf16[8,512,256]{2,1,0:T(8,128)(2,1)} %get-tuple-element.275, s32[]{:T(128)} %get-tuple-element.263), kind=kOutput, calls=%fused_computation.9.clone.1 | convolution fusion | flops 1075838976 | bytes 12845569 | tf_op jit(solution)/shard_map/while/body/eval_jaxpr/dot_general | solution.py:47
  416.4 4.9 convert_reduce_fusion.3
  421.3 6.8 %convolution_add_fusion.3 = f32[4096,256]{1,0:T(8,128)} fusion(bf16[512,4096]{1,0:T(8,128)(2,1)} %get-tuple-element.228, f32[4096,256]{1,0:T(8,128)} %get-tuple-element.264, pred[]{:T(512)S(6)} %compare.3, bf16[8,512,256]{2,1,0:T(8,128)(2,1)} %get-tuple-element.275, s32[]{:T(128)} %get-tuple-element.263), kind=kOutput, calls=%fused_computation.9.clone.1 | convolution fusion | flops 1075838976 | bytes 12845569 | tf_op jit(solution)/shard_map/while/body/eval_jaxpr/dot_general | solution.py:47
  428.1 4.9 convert_reduce_fusion.3
  432.9 6.8 %convolution_add_fusion.3 = f32[4096,256]{1,0:T(8,128)} fusion(bf16[512,4096]{1,0:T(8,128)(2,1)} %get-tuple-element.228, f32[4096,256]{1,0:T(8,128)} %get-tuple-element.264, pred[]{:T(512)S(6)} %compare.3, bf16[8,512,256]{2,1,0:T(8,128)(2,1)} %get-tuple-element.275, s32[]{:T(128)} %get-tuple-element.263), kind=kOutput, calls=%fused_computation.9.clone.1 | convolution fusion | flops 1075838976 | bytes 12845569 | tf_op jit(solution)/shard_map/while/body/eval_jaxpr/dot_general | solution.py:47
  439.7 4.9 convert_reduce_fusion.3
  444.6 6.8 %convolution_add_fusion.3 = f32[4096,256]{1,0:T(8,128)} fusion(bf16[512,4096]{1,0:T(8,128)(2,1)} %get-tuple-element.228, f32[4096,256]{1,0:T(8,128)} %get-tuple-element.264, pred[]{:T(512)S(6)} %compare.3, bf16[8,512,256]{2,1,0:T(8,128)(2,1)} %get-tuple-element.275, s32[]{:T(128)} %get-tuple-element.263), kind=kOutput, calls=%fused_computation.9.clone.1 | convolution fusion | flops 1075838976 | bytes 12845569 | tf_op jit(solution)/shard_map/while/body/eval_jaxpr/dot_general | solution.py:47
  451.3 4.9 convert_reduce_fusion.3
  456.2 6.8 %convolution_add_fusion.3 = f32[4096,256]{1,0:T(8,128)} fusion(bf16[512,4096]{1,0:T(8,128)(2,1)} %get-tuple-element.228, f32[4096,256]{1,0:T(8,128)} %get-tuple-element.264, pred[]{:T(512)S(6)} %compare.3, bf16[8,512,256]{2,1,0:T(8,128)(2,1)} %get-tuple-element.275, s32[]{:T(128)} %get-tuple-element.263), kind=kOutput, calls=%fused_computation.9.clone.1 | convolution fusion | flops 1075838976 | bytes 12845569 | tf_op jit(solution)/shard_map/while/body/eval_jaxpr/dot_general | solution.py:47
  463.0 4.9 convert_reduce_fusion.3
  467.9 6.8 %convolution_add_fusion.3 = f32[4096,256]{1,0:T(8,128)} fusion(bf16[512,4096]{1,0:T(8,128)(2,1)} %get-tuple-element.228, f32[4096,256]{1,0:T(8,128)} %get-tuple-element.264, pred[]{:T(512)S(6)} %compare.3, bf16[8,512,256]{2,1,0:T(8,128)(2,1)} %get-tuple-element.275, s32[]{:T(128)} %get-tuple-element.263), kind=kOutput, calls=%fused_computation.9.clone.1 | convolution fusion | flops 1075838976 | bytes 12845569 | tf_op jit(solution)/shard_map/while/body/eval_jaxpr/dot_general | solution.py:47
  474.6 4.9 convert_reduce_fusion.3
  479.5 6.8 %convolution_add_fusion.3 = f32[4096,256]{1,0:T(8,128)} fusion(bf16[512,4096]{1,0:T(8,128)(2,1)} %get-tuple-element.228, f32[4096,256]{1,0:T(8,128)} %get-tuple-element.264, pred[]{:T(512)S(6)} %compare.3, bf16[8,512,256]{2,1,0:T(8,128)(2,1)} %get-tuple-element.275, s32[]{:T(128)} %get-tuple-element.263), kind=kOutput, calls=%fused_computation.9.clone.1 | convolution fusion | flops 1075838976 | bytes 12845569 | tf_op jit(solution)/shard_map/while/body/eval_jaxpr/dot_general | solution.py:47
  491.4 55.0 %all-reduce = f32[4096]{0:T(1024)S(1)} all-reduce(f32[4096]{0:T(1024)S(1)} %get-tuple-element.76), channel_id=4, replica_groups=mesh['dp'=4,'code'=32] {'dp'}, use_global_device_ids=true, to_apply=%region_14.15.clone | all-reduce | flops 4096 | bytes 32768
  547.7 25.9 %reduce-scatter.2.cloned.1.call-done = f32[1024,256]{1,0:T(8,128)} async-done(((f32[4096,256]{1,0:T(8,128)}), f32[1024,256]{1,0:T(8,128)}) %reduce-scatter.2.cloned.1.call-update) | async-done | bytes 1048592 | tf_op jit(solution)/shard_map/reduce_scatter | solution.py:98
  573.6 2.8 add_divide_fusion
  (106 shorter events, 55.0 us)
Async XLA Ops:
  7.2 31.3 %copy-start = (bf16[1024,256]{1,0:T(8,128)(2,1)S(1)}, bf16[1024,256]{1,0:T(8,128)(2,1)}, u32[]{:S(2)}) copy-start(bf16[1024,256]{1,0:T(8,128)(2,1)} %param.14) | copy-start | bytes 1572868
  7.2 122.0 %all-gather.3.cloned.1.call-start = ((), (), s32[]{:S(2)}) async-start(), calls=%async_computation.1 | async-start | bytes 2162688 | tf_op jit(solution)/shard_map/all_gather | solution.py:86
  38.5 20.1 %copy-start.2 = (bf16[4096,256]{1,0:T(8,128)(2,1)S(1)}, bf16[4096,256]{1,0:T(8,128)(2,1)}, u32[]{:S(2)}) copy-start(bf16[4096,256]{1,0:T(8,128)(2,1)} %param.15) | copy-start | bytes 6291460
  57.6 516.0 %reduce-scatter.2.cloned.1.call-start = ((), (), s32[]{:S(2)}) async-start(), calls=%async_computation.2 | async-start | bytes 5242880 | tf_op jit(solution)/shard_map/reduce_scatter | solution.py:98
  58.6 1.6 copy-start.3
  486.3 1.6 copy-start.4
  487.9 2.3 copy-start.5
  487.9 88.6 %copy-start.1 = (bf16[1024,256]{1,0:T(8,128)(2,1)S(1)}, bf16[1024,256]{1,0:T(8,128)(2,1)}, u32[]{:S(2)}) copy-start(bf16[1024,256]{1,0:T(8,128)(2,1)} %param.14) | copy-start | bytes 1572868
Sparse Core Ops, SparseCore 0:
  57.7 71.4 all-gather.2
  486.4 87.1 reduce-scatter.1
